TPU v7x, 32 devices: a whole 2x2x4 slice. The times are simulated.
32 devices in a mesh: groups: 2 (over y), seq: 4 (over z), inner: 2 (over x), head: 2 (over core).
Axes of the slice: x: 2, y: 2, z: 4, core: 2. Of those that a mesh axis runs over, the one named last changes fastest.
Arguments:
- queries: bfloat16 [2048, 32, 128], P(('groups', 'seq', 'inner'), 'head'), parts along dimension 0, as said below
- keys: bfloat16 [2048, 4, 128], P(('groups', 'seq', 'inner'), 'head'), parts along dimension 0
- values: bfloat16 [2048, 4, 128], P(('groups', 'seq', 'inner'), 'head'), parts along dimension 0, may hold values from -6 to 6
- log_decay: float32 [2048, 4], P(('groups', 'seq', 'inner'), 'head'), parts along dimension 0, as said below
- gain: float32 [32, 128], P('head'), may hold values from 0.1 to 1.9
- block_list: int32 [32, 16], P(('groups', 'seq', 'inner')), parts along dimension 0, may hold values from 0 to 15, as said below
Outputs:
- attended: bfloat16 [2048, 32, 128], P(('groups', 'seq', 'inner'), 'head'), parts along dimension 0
There are 2 independent parts, one for each index of `groups`. A program takes and returns all parts, laid end to end along the dimension named above; an argument that names none is the same for every part. Nothing has to cross between parts.
Inputs may be any that keep to these rules, and one draw needn't show every extreme that they name: Keys lie within -6 to 6; queries within -144 to 144. `log_decay`: each entry is below 0. `block_list`: entry 0 of row b is b. The sequence's pieces of 128 tokens fall into segments: piece p belongs to segment p modulo 2. Every entry of row b is a block at or before b in a piece of b's segment.
All inputs are finite; a program needn't handle non-finite values.
Results may differ from a plain program's by a relative error of at most 0.0017.
Values may be sent and summed in bfloat16 or wider, within the bound.
A program may use at most 64 MiB of HBM per device.

v0:
```python
import functools

import jax
import jax.numpy as jnp
from jax import lax
from jax.experimental import pallas as pl
from jax.experimental.pallas import tpu as pltpu
from jax.sharding import PartitionSpec as P

BLK = 64
HIGH = lax.Precision.HIGHEST
MESH = pl.DeviceIdType.MESH
LD_ROWS = 8
F32 = jnp.float32
BF16 = jnp.bfloat16
LOG2E = 1.4426950408889634


def iota(shape, dim):
    return lax.broadcasted_iota(jnp.int32, shape, dim)


def dot(a, b, dims=((1,), (0,)), precision=None):
    return lax.dot_general(
        a, b, (dims, ((), ())), precision=precision, preferred_element_type=F32
    )


def halves(x):
    hi = x.astype(BF16)
    return hi, (x - hi.astype(F32)).astype(BF16)


def kernel(
    n_seq, n_inner, kv,
    q_hbm, k_hbm, v_hbm, ld_hbm, gain_ref, list_ref,
    out_ref,
    qbuf, kbuf, vbuf, ldbuf, qs, kd, vd, bias, lin, sp, msg, got, own_msg, own_got,
    local_sem, k_send, k_recv, v_send, v_recv, l_send, l_recv, x_send, x_recv,
    m_send, m_recv, o_send, o_recv,
):
    z = lax.axis_index("seq")
    x = lax.axis_index("inner")
    tokens, heads, width = qbuf.shape
    rep = heads // kv
    rows = tokens * rep
    per_piece = tokens // BLK
    keys_all = n_seq * tokens
    has_next, has_last = z < n_seq - 1, z > 0

    ldbuf[...] = jnp.zeros_like(ldbuf)
    q_copy = pltpu.make_async_copy(q_hbm, qbuf, local_sem.at[0])
    k_copy = pltpu.make_async_copy(k_hbm, kbuf.at[0], local_sem.at[1])
    v_copy = pltpu.make_async_copy(v_hbm, vbuf.at[0], local_sem.at[2])
    l_copy = pltpu.make_async_copy(ld_hbm, ldbuf.at[0, 0, 0:kv], local_sem.at[3])
    for copy in (l_copy, k_copy, v_copy, q_copy):
        copy.start()

    barrier = pltpu.get_barrier_semaphore()

    @pl.when(has_next)
    def _():
        pl.semaphore_signal(barrier, inc=1, device_id={"seq": z + 1}, device_id_type=MESH)

    @pl.when(has_last)
    def _():
        pl.semaphore_signal(barrier, inc=1, device_id={"seq": z - 1}, device_id_type=MESH)

    for o in range(1, n_inner):
        pl.semaphore_signal(
            barrier, inc=1, device_id={"inner": lax.rem(x + o, n_inner)}, device_id_type=MESH)
    ends = jnp.where(has_next, 1, 0) + jnp.where(has_last, 1, 0)
    pl.semaphore_wait(barrier, n_inner - 1 + ends)

    def hop(src, dst, send, recv):
        return pltpu.make_async_remote_copy(
            src_ref=src, dst_ref=dst, send_sem=send, recv_sem=recv,
            device_id={"seq": z + 1}, device_id_type=MESH)

    def k_hop(j):
        return hop(
            k_hbm if j == 0 else kbuf.at[j], kbuf.at[j + 1], k_send.at[j], k_recv.at[j + 1])

    def v_hop(j):
        return hop(
            v_hbm if j == 0 else vbuf.at[j], vbuf.at[j + 1], v_send.at[j], v_recv.at[j + 1])

    def l_hop(j):
        return hop(
            ldbuf.at[j, :, 0:kv], ldbuf.at[j + 1, :, 0:kv], l_send.at[j], l_recv.at[j + 1])

    def relay(hops, j):
        @pl.when(z >= j)
        def _():
            hops(j - 1).wait_recv()

        if j < n_seq - 1:

            @pl.when((z >= j) & has_next)
            def _():
                hops(j).start()

    def x_copy(o):
        return pltpu.make_async_remote_copy(
            src_ref=ld_hbm, dst_ref=ldbuf.at[0, n_inner - o, 0:kv], send_sem=x_send.at[o],
            recv_sem=x_recv.at[o], device_id={"inner": lax.rem(x + o, n_inner)},
            device_id_type=MESH)

    @pl.when(has_next)
    def _():
        k_hop(0).start()
        v_hop(0).start()

    for o in range(1, n_inner):
        x_copy(o).start()

    lanes = iota((kv * tokens, kv * tokens), 1)
    subs = iota((kv * tokens, kv * tokens), 0)
    by_head = jnp.where(
        lanes == lax.rem(subs, tokens) * kv + subs // tokens, 1.0, 0.0
    ).astype(BF16)

    l_copy.wait()
    ld = ldbuf[0, 0]
    upto = jnp.where(iota((tokens, tokens), 0) <= iota((tokens, tokens), 1), 1.0, 0.0)
    after = jnp.where(iota((tokens, tokens), 0) < iota((tokens, tokens), 1), 1.0, 0.0)
    cum_lane = dot(ld, upto, precision=HIGH)
    row_tok = iota((rows, tokens), 0) // rep
    lane_tok = iota((rows, tokens), 1)
    seen = row_tok >= lane_tok
    cum_row = dot(jnp.where(seen, 1.0, 0.0), ld, ((1,), (1,)), HIGH)
    own_tail = dot(after, ld, ((1,), (1,)), HIGH)

    def outer(k, weighted):
        hi, lo = halves(weighted)
        return dot(
            jnp.concatenate([k, k], axis=0), jnp.concatenate([hi, lo], axis=0), ((0,), (0,)))

    def split(j):
        k_j = dot(by_head, kbuf[j]).astype(BF16)
        v_j = dot(by_head, vbuf[j])
        out = []
        for g in range(kv):
            k_g = k_j[g * tokens:(g + 1) * tokens]
            v_g = v_j[g * tokens:(g + 1) * tokens]
            kd[g, j * tokens:(j + 1) * tokens, :] = k_g
            vd[g, j * tokens:(j + 1) * tokens, :] = v_g.astype(BF16)
            out.append((k_g, v_g))
        return out

    k_copy.wait()
    v_copy.wait()
    mine = split(0)
    own = [outer(k_g, v_g * jnp.exp(own_tail[:, g:g + 1])) for g, (k_g, v_g) in enumerate(mine)]
    for g in range(kv):
        own_msg[g] = own[g]

    def o_copy(o):
        return pltpu.make_async_remote_copy(
            src_ref=own_msg, dst_ref=own_got.at[o], send_sem=o_send.at[o],
            recv_sem=o_recv.at[o], device_id={"inner": lax.rem(x + o, n_inner)},
            device_id_type=MESH)

    for o in range(1, n_inner):
        x_copy(o).wait_recv()

    @pl.when(has_next)
    def _():
        l_hop(0).start()

    for o in range(1, n_inner):
        o_copy(o).start()

    def visibility():
        key_lane = iota((1, keys_all), 1)
        key_block = (
            ((z - key_lane // tokens) * n_inner + x) * per_piece + lax.rem(key_lane, tokens) // BLK
        )
        key_pos = key_block * BLK + lax.rem(key_lane, BLK)
        listed = list_ref[...]
        for b in range(per_piece):
            member = key_block == listed[b:b + 1, 0:1]
            for i in range(1, listed.shape[1]):
                member = jnp.logical_or(member, key_block == listed[b:b + 1, i:i + 1])
            limit = jnp.where(member, key_pos, jnp.int32(2**30))
            first = (z * n_inner + x) * tokens + b * BLK
            query = first + iota((BLK * rep, 1), 0) // rep
            bias[b * BLK * rep:(b + 1) * BLK * rep, :] = jnp.where(limit <= query, 0.0, -1e30)

    def take_queries():
        q_copy.wait()
        qf = qbuf[...].astype(F32)
        for g in range(kv):
            qs[g] = qf[:, g * rep:(g + 1) * rep, :].reshape(rows, width).astype(BF16)

    def within(g):
        k_g, v_g = mine[g][0], mine[g][1].astype(BF16)
        diff = cum_row[:, g:g + 1] - cum_lane[g:g + 1, :]
        weight = jnp.where(seen, jnp.exp(jnp.minimum(diff, 0.0)), 0.0)
        hi, lo = halves(dot(qs[g], k_g, ((1,), (1,))) * weight)
        lin[g] = dot(
            jnp.concatenate([hi, lo], axis=1), jnp.concatenate([v_g, v_g], axis=0))

    state = [jnp.zeros((width, width), F32) for _ in range(kv)]
    gap = [jnp.zeros((1, 1), F32) for _ in range(kv)]

    def totals(j):
        t = jnp.sum(ldbuf[j].reshape(n_inner * LD_ROWS, tokens), axis=1, keepdims=True)
        return [[t[o * LD_ROWS + g:o * LD_ROWS + g + 1, :] for o in range(n_inner)]
                for g in range(kv)]

    def absorb(j):
        row = totals(j)
        tail = dot(after, ldbuf[j, 0], ((1,), (1,)), HIGH)
        for g, (k_g, v_g) in enumerate(split(j)):
            rest = gap[g]
            for o in range(1, n_inner):
                rest = rest + jnp.where(x + o < n_inner, row[g][o], 0.0)
            state[g] = state[g] + outer(k_g, v_g * jnp.exp(tail[:, g:g + 1] + rest))
            gap[g] = gap[g] + sum(row[g])

    def first_head():
        take_queries()
        within(0)

    work = [visibility, first_head] + [functools.partial(within, g) for g in range(1, kv)]
    for j in range(1, n_seq):

        @pl.when(z < j)
        def _():
            kbuf[j] = jnp.zeros_like(kbuf[j])
            vbuf[j] = jnp.zeros_like(vbuf[j])

        relay(k_hop, j)
        if work:
            work.pop(0)()
        relay(v_hop, j)
        relay(l_hop, j)
        work.append(functools.partial(absorb, j))
        work.pop(0)()
    for item in work:
        item()

    row = totals(0)
    before = []
    for g in range(kv):
        past, ahead = jnp.zeros((1, 1), F32), jnp.zeros((1, 1), F32)
        for o in range(1, n_inner):
            past = past + jnp.where(x + o >= n_inner, row[g][o], 0.0)
            ahead = ahead + jnp.where(x + o < n_inner, row[g][o], 0.0)
        before.append(past)
        msg[g] = state[g] * jnp.exp(sum(row[g])) + own[g] * jnp.exp(ahead)

    def m_copy(o):
        return pltpu.make_async_remote_copy(
            src_ref=msg, dst_ref=got.at[o], send_sem=m_send.at[o], recv_sem=m_recv.at[o],
            device_id={"seq": z + 1, "inner": lax.rem(x + o, n_inner)}, device_id_type=MESH)

    @pl.when(has_next)
    def _():
        for o in range(1, n_inner):
            m_copy(o).start()

    step = min(rows, 512)
    scale = width ** (-0.5) * LOG2E

    @pl.loop(0, rows // step, unroll=True)
    def _(c):
        at = pl.ds(pl.multiple_of(c * step, step), step)
        for g in range(kv):
            score = dot(qs[g, at, :], kd[g], ((1,), (1,))) + bias[at, :]
            top = jnp.max(score, axis=1, keepdims=True)
            expo = jnp.exp2((score - top) * scale)
            denom = jnp.sum(expo, axis=1, keepdims=True)
            sp[g, at, :] = dot(expo.astype(BF16), vd[g]) / denom


    @pl.when(has_last)
    def _():
        for o in range(1, n_inner):
            m_copy(o).wait_recv()

    @pl.when(z == 0)
    def _():
        got[...] = jnp.zeros_like(got)

    prior = []
    for g in range(kv):
        at_row = state[g]
        for o in range(1, n_inner):
            at_row = at_row + got[o, g]
        prior.append(at_row * jnp.exp(before[g]))
    for o in range(1, n_inner):
        o_copy(o).wait_recv()
        for g in range(kv):
            later = jnp.zeros((1, 1), F32)
            for r in range(n_inner - o + 1, n_inner):
                later = later + row[g][r]
            prior[g] = prior[g] + own_got[o, g] * jnp.where(x >= o, jnp.exp(later), 0.0)

    done = []
    for g in range(kv):
        hi, lo = halves(prior[g])
        q_g = qs[g]
        inter = dot(
            jnp.concatenate([q_g, q_g], axis=1), jnp.concatenate([hi, lo], axis=0))
        linear = lin[g] + inter * jnp.exp(cum_row[:, g:g + 1])
        norm = lax.rsqrt(jnp.mean(linear * linear, axis=1, keepdims=True) + 1e-6)
        scaled = (linear * norm).reshape(tokens, rep, width) * gain_ref[g * rep:(g + 1) * rep, :][None]
        done.append(scaled + sp[g].reshape(tokens, rep, width))
    out_ref[...] = jnp.concatenate(done, axis=1).astype(out_ref.dtype)

    for j in range(n_seq - 1):

        @pl.when((z >= j) & has_next)
        def _():
            for hops in (k_hop, v_hop, l_hop):
                hops(j).wait_send()

    for o in range(1, n_inner):
        x_copy(o).wait_send()
        o_copy(o).wait_send()

    @pl.when(has_next)
    def _():
        for o in range(1, n_inner):
            m_copy(o).wait_send()


def shards(n_seq, n_inner, queries, keys, values, log_decay, gain, block_list):
    tokens, heads, width = queries.shape
    kv = keys.shape[1]
    rows = tokens * (heads // kv)
    vmem = pl.BlockSpec(memory_space=pltpu.VMEM)
    anywhere = pl.BlockSpec(memory_space=pl.ANY)
    dma = pltpu.SemaphoreType.DMA
    return pl.pallas_call(
        functools.partial(kernel, n_seq, n_inner, kv),
        out_shape=jax.ShapeDtypeStruct(queries.shape, queries.dtype),
        in_specs=[anywhere, anywhere, anywhere, anywhere, vmem, vmem],
        out_specs=vmem,
        scratch_shapes=[
            pltpu.VMEM(queries.shape, BF16),
            pltpu.VMEM((n_seq, kv * tokens, width), BF16),
            pltpu.VMEM((n_seq, kv * tokens, width), BF16),
            pltpu.VMEM((n_seq, n_inner, LD_ROWS, tokens), F32),
            pltpu.VMEM((kv, rows, width), BF16),
            pltpu.VMEM((kv, n_seq * tokens, width), BF16),
            pltpu.VMEM((kv, n_seq * tokens, width), BF16),
            pltpu.VMEM((rows, n_seq * tokens), F32),
            pltpu.VMEM((kv, rows, width), F32),
            pltpu.VMEM((kv, rows, width), F32),
            pltpu.VMEM((kv, width, width), F32),
            pltpu.VMEM((n_inner, kv, width, width), F32),
            pltpu.VMEM((kv, width, width), F32),
            pltpu.VMEM((n_inner, kv, width, width), F32),
            dma((4,)),
            dma((n_seq,)), dma((n_seq,)), dma((n_seq,)), dma((n_seq,)),
            dma((n_seq,)), dma((n_seq,)), dma((n_inner,)), dma((n_inner,)),
            dma((n_inner,)), dma((n_inner,)), dma((n_inner,)), dma((n_inner,)),
        ],
        compiler_params=pltpu.CompilerParams(collective_id=0, has_side_effects=True),
        name="prefill",
    )(
        queries, keys.reshape(tokens * kv, width), values.reshape(tokens * kv, width),
        log_decay.T, gain, block_list,
    )


def solution(mesh):
    return jax.shard_map(
        functools.partial(shards, mesh.shape["seq"], mesh.shape["inner"]),
        mesh=mesh,
        in_specs=(
            P(("groups", "seq", "inner"), "head", None),
            P(("groups", "seq", "inner"), "head", None),
            P(("groups", "seq", "inner"), "head", None),
            P(("groups", "seq", "inner"), "head"),
            P("head", None),
            P(("groups", "seq", "inner"), None),
        ),
        out_specs=P(("groups", "seq", "inner"), "head", None),
        check_vma=False,
    )
```

profile of v0, /device:TPU:24, one launch (start us, length us, event | category | flops | bytes accessed | tf_op | source)
XLA Modules:
  0.0 20.9 jit_solution(10786717348841831084)
XLA Ops:
  0.0 19.0 %prefill.1 = bf16[128,16,128]{2,1,0:T(8,128)(2,1)} custom-call(bf16[128,16,128]{2,1,0:T(8,128)(2,1)} %q_hbm.1, bf16[256,128]{1,0:T(8,128)(2,1)} %bitcast.3, bf16[256,128]{1,0:T(8,128)(2,1)} %bitcast.4, f32[2,128]{1,0:T(2,128)} %bitcast.5, f32[16,128]{1,0:T(8,128)} %gain_ref.1, s32[2,16]{1,0:T(2,128)} %list_ref.1), custom_call_target="tpu_custom_call" | custom-call | tf_op jit(solution)/shard_map/prefill/pallas_call | solution.py:337
  19.0 1.9 %copy.8 = bf16[128,16,128]{2,1,0:T(8,128)(2,1)} copy(bf16[128,16,128]{2,1,0:T(8,128)(2,1)} %prefill.1) | data formatting | bytes 1048576
where the time goes:
time: 21.1 us; the launch traced here: 20.9 us
  Pallas kernels  19 us (90%)
  local copies, waits for them, and re-layouts  1.87 us (9%)
    pallas_call x1, Pallas kernels, shards(): pl.pallas_call(functools.partial(kernel, n_seq, n_inner, kv), out_shape=j...  19 us
    unnamed x1, local copies, waits for them, and re-layouts  1.87 us

commit v1 on v0

--- a/solution.py
+++ b/solution.py
@@ -33,9 +33,9 @@
 
 def kernel(
     n_seq, n_inner, kv,
-    q_hbm, k_hbm, v_hbm, ld_hbm, gain_ref, list_ref,
+    q_hbm, k_hbm, v_hbm, ld_hbm, gain_hbm, list_hbm,
     out_ref,
-    qbuf, kbuf, vbuf, ldbuf, qs, kd, vd, bias, lin, sp, msg, got, own_msg, own_got,
+    gain_ref, list_ref, qbuf, kbuf, vbuf, ldbuf, qs, kd, vd, bias, lin, sp, msg, got, own_msg, own_got,
     local_sem, k_send, k_recv, v_send, v_recv, l_send, l_recv, x_send, x_recv,
     m_send, m_recv, o_send, o_recv,
 ):
@@ -48,15 +48,15 @@
     keys_all = n_seq * tokens
     has_next, has_last = z < n_seq - 1, z > 0
 
-    ldbuf[...] = jnp.zeros_like(ldbuf)
     q_copy = pltpu.make_async_copy(q_hbm, qbuf, local_sem.at[0])
     k_copy = pltpu.make_async_copy(k_hbm, kbuf.at[0], local_sem.at[1])
     v_copy = pltpu.make_async_copy(v_hbm, vbuf.at[0], local_sem.at[2])
     l_copy = pltpu.make_async_copy(ld_hbm, ldbuf.at[0, 0, 0:kv], local_sem.at[3])
-    for copy in (l_copy, k_copy, v_copy, q_copy):
-        copy.start()
+    g_copy = pltpu.make_async_copy(gain_hbm, gain_ref, local_sem.at[4])
+    list_copy = pltpu.make_async_copy(list_hbm, list_ref, local_sem.at[5])
 
     barrier = pltpu.get_barrier_semaphore()
+    ldbuf[...] = jnp.zeros_like(ldbuf)
 
     @pl.when(has_next)
     def _():
@@ -69,6 +69,8 @@
     for o in range(1, n_inner):
         pl.semaphore_signal(
             barrier, inc=1, device_id={"inner": lax.rem(x + o, n_inner)}, device_id_type=MESH)
+    for copy in (l_copy, k_copy, v_copy, list_copy, q_copy, g_copy):
+        copy.start()
     ends = jnp.where(has_next, 1, 0) + jnp.where(has_last, 1, 0)
     pl.semaphore_wait(barrier, n_inner - 1 + ends)
 
@@ -177,6 +179,7 @@
             ((z - key_lane // tokens) * n_inner + x) * per_piece + lax.rem(key_lane, tokens) // BLK
         )
         key_pos = key_block * BLK + lax.rem(key_lane, BLK)
+        list_copy.wait()
         listed = list_ref[...]
         for b in range(per_piece):
             member = key_block == listed[b:b + 1, 0:1]
@@ -298,6 +301,7 @@
                 later = later + row[g][r]
             prior[g] = prior[g] + own_got[o, g] * jnp.where(x >= o, jnp.exp(later), 0.0)
 
+    g_copy.wait()
     done = []
     for g in range(kv):
         hi, lo = halves(prior[g])
@@ -336,10 +340,12 @@
     dma = pltpu.SemaphoreType.DMA
     return pl.pallas_call(
         functools.partial(kernel, n_seq, n_inner, kv),
-        out_shape=jax.ShapeDtypeStruct(queries.shape, queries.dtype),
-        in_specs=[anywhere, anywhere, anywhere, anywhere, vmem, vmem],
+        out_shape=pltpu.VMEM(queries.shape, queries.dtype),
+        in_specs=[anywhere] * 6,
         out_specs=vmem,
         scratch_shapes=[
+            pltpu.VMEM(gain.shape, F32),
+            pltpu.VMEM(block_list.shape, jnp.int32),
             pltpu.VMEM(queries.shape, BF16),
             pltpu.VMEM((n_seq, kv * tokens, width), BF16),
             pltpu.VMEM((n_seq, kv * tokens, width), BF16),
@@ -354,7 +360,7 @@
             pltpu.VMEM((n_inner, kv, width, width), F32),
             pltpu.VMEM((kv, width, width), F32),
             pltpu.VMEM((n_inner, kv, width, width), F32),
-            dma((4,)),
+            dma((6,)),
             dma((n_seq,)), dma((n_seq,)), dma((n_seq,)), dma((n_seq,)),
             dma((n_seq,)), dma((n_seq,)), dma((n_inner,)), dma((n_inner,)),
             dma((n_inner,)), dma((n_inner,)), dma((n_inner,)), dma((n_inner,)),

time: 21.1 us -> 18.4 us (0.87)
  Pallas kernels: 19 us -> 17.5 us
  local copies, waits for them, and re-layouts: 1.87 us -> 0.8 us
    pallas_call x1, Pallas kernels: 19 us -> 17.5 us  [shards(): pl.pallas_call(functools.partial(kernel, n_seq, n_inner, kv), out_shape=p...]
    unnamed x1, local copies, waits for them, and re-layouts: 1.87 us -> 0.8 us
where the time goes in v1:
time: 18.4 us; the launch traced here: 18.3 us
  Pallas kernels  17.5 us (95%)
  local copies, waits for them, and re-layouts  0.8 us (4%)
    pallas_call x1, Pallas kernels, shards(): pl.pallas_call(functools.partial(kernel, n_seq, n_inner, kv), out_shape=p...  17.5 us
    unnamed x1, local copies, waits for them, and re-layouts  0.8 us

profile of v1, /device:TPU:24, one launch (start us, length us, event | category | flops | bytes accessed | tf_op | source)
XLA Modules:
  0.0 18.3 jit_solution(3319798136852174764)
XLA Ops:
  0.0 17.5 %prefill.1 = bf16[128,16,128]{2,1,0:T(8,128)(2,1)S(1)} custom-call(bf16[128,16,128]{2,1,0:T(8,128)(2,1)} %q_hbm.1, bf16[256,128]{1,0:T(8,128)(2,1)} %bitcast.3, bf16[256,128]{1,0:T(8,128)(2,1)} %bitcast.4, f32[2,128]{1,0:T(2,128)} %bitcast.5, f32[16,128]{1,0:T(8,128)} %gain_hbm.1, s32[2,16]{1,0:T(2,128)} %list_hbm.1), custom_call_target="tpu_custom_call" | custom-call | tf_op jit(solution)/shard_map/prefill/pallas_call | solution.py:341
  17.5 0.8 %copy.8 = bf16[128,16,128]{2,1,0:T(8,128)(2,1)} copy(bf16[128,16,128]{2,1,0:T(8,128)(2,1)S(1)} %prefill.1) | data formatting | bytes 1048576

commit v2 on v1

v2 whole, which is shorter than its diff:
```python
import functools

import jax
import jax.numpy as jnp
from jax import lax
from jax.experimental import pallas as pl
from jax.experimental.pallas import tpu as pltpu
from jax.sharding import PartitionSpec as P

BLK = 64
HIGH = lax.Precision.HIGHEST
MESH = pl.DeviceIdType.MESH
LD_ROWS = 8
F32 = jnp.float32
BF16 = jnp.bfloat16
LOG2E = 1.4426950408889634
NEVER = -1e30


def iota(shape, dim):
    return lax.broadcasted_iota(jnp.int32, shape, dim)


def dot(a, b, dims=((1,), (0,)), precision=None):
    return lax.dot_general(
        a, b, (dims, ((), ())), precision=precision, preferred_element_type=F32
    )


def halves(x):
    hi = x.astype(BF16)
    return hi, (x - hi.astype(F32)).astype(BF16)


def thirds(x):
    hi = x.astype(BF16)
    rest = x - hi.astype(F32)
    mid = rest.astype(BF16)
    return hi, mid, (rest - mid.astype(F32)).astype(BF16)


def kernel(
    n_seq, n_inner, kv, parts,
    q_hbm, k_hbm, v_hbm, ld_hbm, gain_hbm, list_hbm,
    out_ref,
    gain_ref, list_ref, qbuf, kbuf, vbuf, kx, vx, ldbuf, qs, kd, vd, vis, wmat, emat,
    score, prob, inv, lin, sp, state,
    local_sem, k_send, k_recv, v_send, v_recv, l_send, l_recv, x_send, x_recv,
    kx_send, kx_recv, vx_send, vx_recv,
):
    z = lax.axis_index("seq")
    x = lax.axis_index("inner")
    tokens, heads, width = qbuf.shape
    rep = heads // kv
    rows = tokens * rep
    pairs = tokens * kv
    per_piece = tokens // BLK
    keys_all = n_seq * tokens
    has_next, has_last = z < n_seq - 1, z > 0
    others = range(1, n_inner)

    barrier = pltpu.get_barrier_semaphore()

    ldbuf[...] = jnp.zeros_like(ldbuf)

    @pl.when(has_last)
    def _():
        pl.semaphore_signal(barrier, inc=1, device_id={"seq": z - 1}, device_id_type=MESH)

    for o in others:
        pl.semaphore_signal(
            barrier, inc=1, device_id={"inner": lax.rem(x + o, n_inner)}, device_id_type=MESH)

    q_copy = pltpu.make_async_copy(q_hbm, qbuf, local_sem.at[0])
    k_copy = pltpu.make_async_copy(k_hbm, kbuf.at[0], local_sem.at[1])
    v_copy = pltpu.make_async_copy(v_hbm, vbuf.at[0], local_sem.at[2])
    l_copy = pltpu.make_async_copy(ld_hbm, ldbuf.at[0, 0, 0:kv], local_sem.at[3])
    g_copy = pltpu.make_async_copy(gain_hbm, gain_ref, local_sem.at[4])
    list_copy = pltpu.make_async_copy(list_hbm, list_ref, local_sem.at[5])
    for copy in (l_copy, k_copy, v_copy, q_copy, list_copy, g_copy):
        copy.start()
    pl.semaphore_wait(barrier, n_inner - 1 + jnp.where(has_next, 1, 0))

    def hop(src, dst, send, recv):
        return pltpu.make_async_remote_copy(
            src_ref=src, dst_ref=dst, send_sem=send, recv_sem=recv,
            device_id={"seq": z + 1}, device_id_type=MESH)

    def across(o, src, dst, send, recv):
        return pltpu.make_async_remote_copy(
            src_ref=src, dst_ref=dst, send_sem=send, recv_sem=recv,
            device_id={"inner": lax.rem(x + o, n_inner)}, device_id_type=MESH)

    span = pairs // parts

    def part(ref, c):
        return ref.at[pl.ds(c * span, span)]

    def k_of(j):
        return k_hbm if j == 0 else kbuf.at[j]

    def v_of(j, c):
        return part(v_hbm if j == 0 else vbuf.at[j], c)

    def k_hop(j):
        return hop(k_of(j), kbuf.at[j + 1], k_send.at[j], k_recv.at[j + 1])

    def v_hop(j, c):
        return hop(v_of(j, c), part(vbuf.at[j + 1], c), v_send.at[j, c], v_recv.at[j + 1, c])

    def l_hop(j):
        return hop(
            ldbuf.at[j, :, 0:kv], ldbuf.at[j + 1, :, 0:kv], l_send.at[j], l_recv.at[j + 1])

    def k_across(o, j):
        s = n_inner - o
        return across(o, k_of(j), kx.at[s - 1, j], kx_send.at[o, j], kx_recv.at[s, j])

    def v_across(o, j, c):
        s = n_inner - o
        return across(
            o, v_of(j, c), part(vx.at[s - 1, j], c), vx_send.at[o, j, c], vx_recv.at[s, j, c])

    def x_copy(o):
        return across(o, ld_hbm, ldbuf.at[0, n_inner - o, 0:kv], x_send.at[o], x_recv.at[o])

    def relay(hops, j, spread=None):
        @pl.when(z >= j)
        def _():
            hops(j - 1).wait_recv()
            if spread is not None:
                for o in others:
                    spread(o, j).start()

        if j < n_seq - 1:

            @pl.when((z >= j) & has_next)
            def _():
                hops(j).start()

    def relay_k(j):
        relay(k_hop, j, k_across)

    def relay_v(j, c):
        relay(lambda i: v_hop(i, c), j, lambda o, i: v_across(o, i, c))

    @pl.when(has_next)
    def _():
        k_hop(0).start()
        for c in range(parts):
            v_hop(0, c).start()

    for o in others:
        x_copy(o).start()
    for o in others:
        k_across(o, 0).start()
        for c in range(parts):
            v_across(o, 0, c).start()

    for j in range(1, n_seq):

        @pl.when(z < j)
        def _():
            kbuf[j] = jnp.zeros_like(kbuf[j])
            vbuf[j] = jnp.zeros_like(vbuf[j])
            for o in others:
                kx[o - 1, j] = jnp.zeros_like(kx[o - 1, j])
                vx[o - 1, j] = jnp.zeros_like(vx[o - 1, j])

    state[...] = jnp.zeros_like(state)
    by_head = jnp.where(
        iota((pairs, pairs), 1) == lax.rem(iota((pairs, pairs), 0), tokens) * kv
        + iota((pairs, pairs), 0) // tokens, 1.0, 0.0
    ).astype(BF16)
    owner = lax.rem(iota((pairs, 1), 0), kv)
    after = jnp.where(
        iota((pairs, 2 * tokens), 1) > iota((pairs, 2 * tokens), 0) // kv, 1.0, 0.0
    ).astype(BF16)

    l_copy.wait()
    ld = ldbuf[0, 0]
    seen = iota((tokens, tokens), 0) >= iota((tokens, tokens), 1)
    upto = jnp.where(iota((tokens, tokens), 0) <= iota((tokens, tokens), 1), 1.0, 0.0)
    cum_lane = dot(ld, upto, precision=HIGH)
    ld_rows = jnp.concatenate(
        [jnp.broadcast_to(ld[g:g + 1, :], (width, tokens)) for g in range(kv)], axis=0)
    cum_all = dot(jnp.where(seen, 1.0, 0.0), ld_rows, ((1,), (1,)), HIGH)
    for g in range(kv):
        cum = cum_all[:, g * width:(g + 1) * width]
        emat[g] = jnp.exp(cum)
        wmat[g] = jnp.where(
            seen, jnp.exp(jnp.minimum(cum - cum_lane[g:g + 1, :], 0.0)), 0.0)

    def spread_rows(by_token):
        return jnp.broadcast_to(
            by_token[:, None, :], (tokens, rep, by_token.shape[1])
        ).reshape(rows, by_token.shape[1])

    def split(buf, dst, j):
        both = dot(by_head, buf[j]).astype(BF16)
        for g in range(kv):
            dst[g, j * tokens:(j + 1) * tokens, :] = both[g * tokens:(g + 1) * tokens]

    def absorb(k, v, ld_piece, later, valid=None):
        both = jnp.concatenate([ld_piece, later], axis=1)
        tail = sum(dot(after, t, ((1,), (1,))) for t in thirds(both))
        weight = jnp.exp(tail)
        if valid is not None:
            weight = jnp.where(valid, weight, 0.0)
        vf = v.astype(F32)
        weighted = jnp.concatenate(
            [vf * jnp.where(owner == g, weight[:, g:g + 1], 0.0) for g in range(kv)], axis=1)
        hi, lo = halves(weighted)
        state[...] += dot(
            jnp.concatenate([k, k], axis=0), jnp.concatenate([hi, lo], axis=0), ((0,), (0,)))

    def place(s):
        return lax.rem(x + s, n_inner)

    def between(j):
        total = jnp.zeros((LD_ROWS, tokens), F32)
        for s in others:
            total = total + jnp.where(place(s) < x, ldbuf[0, s], 0.0)
        for i in range(1, j):
            for s in range(n_inner):
                total = total + ldbuf[i, s]
        return total

    def absorb_row(j, s):
        if j == 0:
            later = jnp.zeros((LD_ROWS, tokens), F32)
            for r in others:
                later = later + jnp.where(
                    (place(r) > place(s)) & (place(r) < x), ldbuf[0, r], 0.0)
            absorb(kx[s - 1, 0], vx[s - 1, 0], ldbuf[0, s], later, place(s) < x)
            return
        later = between(j)
        for r in range(n_inner):
            if r != s:
                later = later + jnp.where(place(r) > place(s), ldbuf[j, r], 0.0)
        k, v = (kbuf[j], vbuf[j]) if s == 0 else (kx[s - 1, j], vx[s - 1, j])
        absorb(k, v, ldbuf[j, s], later)

    def absorb_others(j):
        for s in others:
            @pl.when(z >= j)
            def _():
                k_across(n_inner - s, j).wait_recv()
                for c in range(parts):
                    v_across(n_inner - s, j, c).wait_recv()
        for s in others:
            absorb_row(j, s)

    def visibility():
        list_copy.wait()
        lane = iota((1, keys_all), 1)
        key_block = (
            ((z - lane // tokens) * n_inner + x) * per_piece + lax.rem(lane, tokens) // BLK
        )
        listed = list_ref[...]
        for b in range(per_piece):
            member = key_block == listed[b:b + 1, 0:1]
            for i in range(1, listed.shape[1]):
                member = jnp.logical_or(member, key_block == listed[b:b + 1, i:i + 1])
            vis[b:b + 1, :] = jnp.where(member, 0.0, NEVER)

    def take_queries():
        q_copy.wait()
        qf = qbuf[...].astype(F32)
        for g in range(kv):
            qs[g] = qf[:, g * rep:(g + 1) * rep, :].reshape(rows, width).astype(BF16)

    half = BLK * rep

    def shown(s, j):
        cut = slice(j * tokens, (j + 1) * tokens)
        return jnp.concatenate(
            [s[b * half:(b + 1) * half] + vis[b:b + 1, cut] for b in range(per_piece)], axis=0)

    def own_piece(g):
        raw = dot(qs[g], kd[g, 0:tokens, :], ((1,), (1,)))
        past = iota((rows, tokens), 0) // rep >= iota((rows, tokens), 1)
        score[g, :, 0:tokens] = jnp.where(past, shown(raw, 0), NEVER)
        hi, lo = halves(raw * spread_rows(wmat[g]))
        v_g = vd[g, 0:tokens, :]
        lin[g] = dot(
            jnp.concatenate([hi, lo], axis=1), jnp.concatenate([v_g, v_g], axis=0))

    def score_piece(j):
        split(kbuf, kd, j)
        for g in range(kv):
            s = dot(qs[g], kd[g, j * tokens:(j + 1) * tokens, :], ((1,), (1,)))
            score[g, :, j * tokens:(j + 1) * tokens] = shown(s, j)

    scale = width ** (-0.5) * LOG2E

    def weigh(g, at):
        s = score[g, at, :]
        top = jnp.max(s, axis=1, keepdims=True)
        expo = jnp.exp2((s - top) * scale)
        denom = jnp.sum(expo, axis=1, keepdims=True)
        prob[g, at, :] = expo.astype(BF16)
        inv[g, at, :] = jnp.broadcast_to(1.0 / denom, (s.shape[0], width))

    k_copy.wait()
    v_copy.wait()
    split(kbuf, kd, 0)
    split(vbuf, vd, 0)
    for o in others:
        x_copy(o).wait_recv()

    @pl.when(has_next)
    def _():
        l_hop(0).start()

    take_queries()
    visibility()
    own_piece(0)

    weighing = [
        functools.partial(weigh, g, slice(b * half, (b + 1) * half))
        for g in range(kv) for b in range(per_piece)
    ]
    for j in range(1, n_seq):
        relay_k(j)
        if j == 1:
            for g in range(1, kv):
                own_piece(g)
        score_piece(j)
        last = j == n_seq - 1
        for c in range(parts):
            if last and weighing:
                weighing.pop(0)()
            relay_v(j, c)
        relay(l_hop, j)
        split(vbuf, vd, j)
        absorb_row(j, 0)
        absorb_others(j - 1)
    for item in weighing:
        item()
    for g in range(kv):
        sp[g] = dot(prob[g], vd[g]) * inv[g]
    g_copy.wait()
    absorb_others(n_seq - 1)

    done = []
    for g in range(kv):
        hi, lo = halves(state[:, g * width:(g + 1) * width])
        q_g = qs[g]
        inter = dot(
            jnp.concatenate([q_g, q_g], axis=1), jnp.concatenate([hi, lo], axis=0))
        linear = lin[g] + inter * spread_rows(emat[g])
        norm = lax.rsqrt(jnp.mean(linear * linear, axis=1, keepdims=True) + 1e-6)
        scaled = (linear * norm).reshape(tokens, rep, width) * gain_ref[g * rep:(g + 1) * rep, :][None]
        done.append(scaled + sp[g].reshape(tokens, rep, width))
    out_ref[...] = jnp.concatenate(done, axis=1).astype(out_ref.dtype)

    for j in range(n_seq - 1):

        @pl.when((z >= j) & has_next)
        def _():
            k_hop(j).wait_send()
            for c in range(parts):
                v_hop(j, c).wait_send()
            l_hop(j).wait_send()

    for o in others:
        x_copy(o).wait_send()
        for j in range(n_seq):

            @pl.when(z >= j)
            def _():
                k_across(o, j).wait_send()
                for c in range(parts):
                    v_across(o, j, c).wait_send()


def shards(n_seq, n_inner, queries, keys, values, log_decay, gain, block_list):
    tokens, heads, width = queries.shape
    kv = keys.shape[1]
    rows = tokens * (heads // kv)
    pairs = tokens * kv
    keys_all = n_seq * tokens
    parts = 4 if n_seq * n_inner <= 16 else 1
    side = max(n_inner - 1, 1)
    anywhere = pl.BlockSpec(memory_space=pl.ANY)
    dma = pltpu.SemaphoreType.DMA
    return pl.pallas_call(
        functools.partial(kernel, n_seq, n_inner, kv, parts),
        out_shape=pltpu.VMEM(queries.shape, queries.dtype),
        in_specs=[anywhere] * 6,
        out_specs=pl.BlockSpec(memory_space=pltpu.VMEM),
        scratch_shapes=[
            pltpu.VMEM(gain.shape, F32),
            pltpu.VMEM(block_list.shape, jnp.int32),
            pltpu.VMEM(queries.shape, BF16),
            pltpu.VMEM((n_seq, pairs, width), BF16),
            pltpu.VMEM((n_seq, pairs, width), BF16),
            pltpu.VMEM((side, n_seq, pairs, width), BF16),
            pltpu.VMEM((side, n_seq, pairs, width), BF16),
            pltpu.VMEM((n_seq, n_inner, LD_ROWS, tokens), F32),
            pltpu.VMEM((kv, rows, width), BF16),
            pltpu.VMEM((kv, keys_all, width), BF16),
            pltpu.VMEM((kv, keys_all, width), BF16),
            pltpu.VMEM((block_list.shape[0], keys_all), F32),
            pltpu.VMEM((kv, tokens, tokens), F32),
            pltpu.VMEM((kv, tokens, width), F32),
            pltpu.VMEM((kv, rows, keys_all), F32),
            pltpu.VMEM((kv, rows, keys_all), BF16),
            pltpu.VMEM((kv, rows, width), F32),
            pltpu.VMEM((kv, rows, width), F32),
            pltpu.VMEM((kv, rows, width), F32),
            pltpu.VMEM((width, kv * width), F32),
            dma((6,)),
            dma((n_seq,)), dma((n_seq,)), dma((n_seq, parts)), dma((n_seq, parts)),
            dma((n_seq,)), dma((n_seq,)), dma((n_inner,)), dma((n_inner,)),
            dma((n_inner, n_seq)), dma((n_inner, n_seq)),
            dma((n_inner, n_seq, parts)), dma((n_inner, n_seq, parts)),
        ],
        compiler_params=pltpu.CompilerParams(collective_id=0, has_side_effects=True),
        name="prefill",
    )(
        queries, keys.reshape(pairs, width), values.reshape(pairs, width),
        log_decay.T, gain, block_list,
    )


def solution(mesh):
    return jax.shard_map(
        functools.partial(shards, mesh.shape["seq"], mesh.shape["inner"]),
        mesh=mesh,
        in_specs=(
            P(("groups", "seq", "inner"), "head", None),
            P(("groups", "seq", "inner"), "head", None),
            P(("groups", "seq", "inner"), "head", None),
            P(("groups", "seq", "inner"), "head"),
            P("head", None),
            P(("groups", "seq", "inner"), None),
        ),
        out_specs=P(("groups", "seq", "inner"), "head", None),
        check_vma=False,
    )
```

time: 18.4 us -> 18.9 us (1.027)
  Pallas kernels: 17.5 us -> 18 us
    pallas_call x1, Pallas kernels: 17.5 us -> 18 us  [shards(): pl.pallas_call(functools.partial(kernel, n_seq, n_inner, kv, parts), out_...]
where the time goes in v2:
time: 18.9 us; the launch traced here: 18.8 us
  Pallas kernels  18 us (95%)
  local copies, waits for them, and re-layouts  0.8 us (4%)
    pallas_call x1, Pallas kernels, shards(): pl.pallas_call(functools.partial(kernel, n_seq, n_inner, kv, parts), out_...  18 us
    unnamed x1, local copies, waits for them, and re-layouts  0.8 us

profile of v2, /device:TPU:24, one launch (start us, length us, event | category | flops | bytes accessed | tf_op | source)
XLA Modules:
  0.0 18.8 jit_solution(16756563594958239291)
XLA Ops:
  0.0 18.0 %prefill.1 = bf16[128,16,128]{2,1,0:T(8,128)(2,1)S(1)} custom-call(bf16[128,16,128]{2,1,0:T(8,128)(2,1)} %q_hbm.1, bf16[256,128]{1,0:T(8,128)(2,1)} %bitcast.3, bf16[256,128]{1,0:T(8,128)(2,1)} %bitcast.4, f32[2,128]{1,0:T(2,128)} %bitcast.5, f32[16,128]{1,0:T(8,128)} %gain_hbm.1, s32[2,16]{1,0:T(2,128)} %list_hbm.1), custom_call_target="tpu_custom_call" | custom-call | tf_op jit(solution)/shard_map/prefill/pallas_call | solution.py:388
  18.0 0.8 %copy.8 = bf16[128,16,128]{2,1,0:T(8,128)(2,1)} copy(bf16[128,16,128]{2,1,0:T(8,128)(2,1)S(1)} %prefill.1) | data formatting | bytes 1048576

commit v3 on v2

v3 whole, which is shorter than its diff:
```python
import functools

import jax
import jax.numpy as jnp
from jax import lax
from jax.experimental import pallas as pl
from jax.experimental.pallas import tpu as pltpu
from jax.sharding import PartitionSpec as P

BLK = 64
HIGH = lax.Precision.HIGHEST
MESH = pl.DeviceIdType.MESH
LD_ROWS = 8
F32 = jnp.float32
BF16 = jnp.bfloat16
LOG2E = 1.4426950408889634
NEVER = -1e30


def iota(shape, dim):
    return lax.broadcasted_iota(jnp.int32, shape, dim)


def dot(a, b, dims=((1,), (0,)), precision=None):
    return lax.dot_general(
        a, b, (dims, ((), ())), precision=precision, preferred_element_type=F32
    )


def halves(x):
    hi = x.astype(BF16)
    return hi, (x - hi.astype(F32)).astype(BF16)


def thirds(x):
    hi = x.astype(BF16)
    rest = x - hi.astype(F32)
    mid = rest.astype(BF16)
    return hi, mid, (rest - mid.astype(F32)).astype(BF16)


def kernel(
    n_seq, n_inner, kv, cuts,
    q_hbm, k_hbm, v_hbm, ld_hbm, gain_hbm, list_hbm,
    out_ref,
    gain_ref, list_ref, qbuf, raw, seg, cross, ldbuf, qs, vis, wmat, emat, cols,
    score, prob, inv, lin, sp, state,
    local_sem, k_recv, v_recv, h_send, l_send, l_recv, x_send, x_recv, c_send, c_recv,
):
    z = lax.axis_index("seq")
    x = lax.axis_index("inner")
    tokens, heads, width = qbuf.shape
    rep = heads // kv
    rows = tokens * rep
    pairs = tokens * kv
    per_piece = tokens // BLK
    keys_all = n_seq * tokens
    has_next, has_last = z < n_seq - 1, z > 0
    others = range(1, n_inner)
    last = n_seq - 1

    barrier = pltpu.get_barrier_semaphore()

    ldbuf[...] = jnp.zeros_like(ldbuf)

    @pl.when(has_last)
    def _():
        pl.semaphore_signal(barrier, inc=1, device_id={"seq": z - 1}, device_id_type=MESH)

    for o in others:
        pl.semaphore_signal(
            barrier, inc=1, device_id={"inner": lax.rem(x + o, n_inner)}, device_id_type=MESH)

    k_copy = pltpu.make_async_copy(k_hbm, raw.at[0], local_sem.at[1])
    v_copy = pltpu.make_async_copy(v_hbm, raw.at[1], local_sem.at[2])
    l_copy = pltpu.make_async_copy(ld_hbm, ldbuf.at[0, 0, 0:kv], local_sem.at[3])
    q_copy = pltpu.make_async_copy(q_hbm, qbuf, local_sem.at[0])
    g_copy = pltpu.make_async_copy(gain_hbm, gain_ref, local_sem.at[4])
    list_copy = pltpu.make_async_copy(list_hbm, list_ref, local_sem.at[5])
    for copy in (l_copy, k_copy, v_copy, q_copy, list_copy, g_copy):
        copy.start()

    by_head = jnp.where(
        iota((pairs, pairs), 1) == lax.rem(iota((pairs, pairs), 0), tokens) * kv
        + iota((pairs, pairs), 0) // tokens, 1.0, 0.0
    ).astype(BF16)
    l_copy.wait()
    k_copy.wait()
    v_copy.wait()
    apart = dot(by_head, jnp.concatenate([raw[0], raw[1]], axis=1)).astype(BF16)
    for i in range(2):
        for g in range(kv):
            seg[0, i, g] = apart[g * tokens:(g + 1) * tokens, i * width:(i + 1) * width]

    pl.semaphore_wait(barrier, n_inner - 1 + jnp.where(has_next, 1, 0))

    def hop(src, dst, send, recv):
        return pltpu.make_async_remote_copy(
            src_ref=src, dst_ref=dst, send_sem=send, recv_sem=recv,
            device_id={"seq": z + 1}, device_id_type=MESH)

    def across(o, src, dst, send, recv):
        return pltpu.make_async_remote_copy(
            src_ref=src, dst_ref=dst, send_sem=send, recv_sem=recv,
            device_id={"inner": lax.rem(x + o, n_inner)}, device_id_type=MESH)

    def part(ref, i, c):
        per_head = cuts[i] // kv
        if per_head == 0:
            return ref.at[i]
        span = tokens // per_head
        return ref.at[i, c // per_head, pl.ds(c % per_head * span, span)]

    def part_hop(j, i, c):
        return hop(
            part(seg.at[j], i, c), part(seg.at[j + 1], i, c), h_send.at[j],
            (k_recv, v_recv)[i].at[j + 1, c])

    def piece_hop(j):
        return hop(seg.at[j], seg.at[j + 1], h_send.at[j], k_recv.at[j + 1, 0])

    def l_hop(j):
        return hop(
            ldbuf.at[j, 0, 0:kv], ldbuf.at[j + 1, 0, 0:kv], l_send.at[j], l_recv.at[j + 1])

    def part_across(o, j, i, c):
        s = n_inner - o
        return across(
            o, part(seg.at[j], i, c), part(cross.at[s - 1, j], i, c), c_send.at[o, j],
            c_recv.at[s, j])

    def piece_across(o, j):
        s = n_inner - o
        return across(o, seg.at[j], cross.at[s - 1, j], c_send.at[o, j], c_recv.at[s, j])

    def l_across(o, j):
        s = n_inner - o
        return across(
            o, ldbuf.at[j, 0, 0:kv], ldbuf.at[j, s, 0:kv], x_send.at[o, j], x_recv.at[s, j])

    def relay_part(j, i, c):
        @pl.when(z >= j)
        def _():
            part_hop(j - 1, i, c).wait_recv()
            if j < last:

                @pl.when(has_next)
                def _():
                    part_hop(j, i, c).start()

            for o in others:
                part_across(o, j, i, c).start()

    def relay_l(j):
        @pl.when(z >= j)
        def _():
            l_hop(j - 1).wait_recv()
            if j < last:

                @pl.when(has_next)
                def _():
                    l_hop(j).start()

            for o in others:
                l_across(o, j).start()

    @pl.when(has_next)
    def _():
        l_hop(0).start()
        for i in range(2):
            for c in range(cuts[i]):
                part_hop(0, i, c).start()

    for o in others:
        l_across(o, 0).start()

        @pl.when(x + o < n_inner)
        def _():
            piece_across(o, 0).start()

    for s in others:

        @pl.when(x + s < n_inner)
        def _():
            cross[s - 1, 0] = jnp.zeros_like(cross[s - 1, 0])

    for j in range(1, n_seq):

        @pl.when(z < j)
        def _():
            seg[j] = jnp.zeros_like(seg[j])
            for o in others:
                cross[o - 1, j] = jnp.zeros_like(cross[o - 1, j])

    def spread_rows(by_token):
        return jnp.broadcast_to(
            by_token[:, None, :], (tokens, rep, by_token.shape[1])
        ).reshape(rows, by_token.shape[1])

    state[...] = jnp.zeros_like(state)
    after = jnp.where(
        iota((tokens, 2 * tokens), 1) > iota((tokens, 2 * tokens), 0), 1.0, 0.0
    ).astype(BF16)

    def decays():
        ld = ldbuf[0, 0]
        seen = iota((tokens, tokens), 0) >= iota((tokens, tokens), 1)
        upto = jnp.where(iota((tokens, tokens), 0) <= iota((tokens, tokens), 1), 1.0, 0.0)
        cum_lane = dot(ld, upto, precision=HIGH)
        ld_rows = jnp.concatenate(
            [jnp.broadcast_to(ld[g:g + 1, :], (width, tokens)) for g in range(kv)], axis=0)
        cum_all = dot(jnp.where(seen, 1.0, 0.0), ld_rows, ((1,), (1,)), HIGH)
        for g in range(kv):
            cum = cum_all[:, g * width:(g + 1) * width]
            emat[g] = spread_rows(jnp.exp(cum))
            wmat[g] = jnp.where(
                seen, jnp.exp(jnp.minimum(cum - cum_lane[g:g + 1, :], 0.0)), 0.0)

    def place(s):
        return lax.rem(x + s, n_inner)

    def later_than(j, s):
        total = jnp.zeros((LD_ROWS, tokens), F32)
        for r in range(n_inner):
            if j == 0 and r > 0:
                total = total + jnp.where(
                    (place(r) > place(s)) & (place(r) < x), ldbuf[0, r], 0.0)
            elif j > 0:
                if r != s:
                    total = total + jnp.where(place(r) > place(s), ldbuf[j, r], 0.0)
                if r > 0:
                    total = total + jnp.where(place(r) < x, ldbuf[0, r], 0.0)
                for i in range(1, j):
                    total = total + ldbuf[i, r]
        return total

    def weigh_pieces(pieces):
        both = jnp.concatenate([
            jnp.concatenate([ldbuf[j, s], later_than(j, s)], axis=1) for j, s in pieces], axis=0)
        tail = dot(
            jnp.concatenate([after] * 3, axis=1), jnp.concatenate(thirds(both), axis=1),
            ((1,), (1,)))
        weight = jnp.exp(tail)
        for n, (j, s) in enumerate(pieces):
            for g in range(kv):
                col = weight[:, n * LD_ROWS + g:n * LD_ROWS + g + 1]
                if j == 0:
                    col = jnp.where(place(s) < x, col, 0.0)
                cols[j % 3, s, g] = jnp.broadcast_to(col, (tokens, width))

    def absorb(pieces):
        for g in range(kv):
            left, right = [], []
            for j, s in pieces:
                piece = seg.at[j] if s == 0 else cross.at[s - 1, j]
                k_g = piece[0, g]
                hi, lo = halves(piece[1, g].astype(F32) * cols[j % 3, s, g])
                left += [k_g, k_g]
                right += [hi, lo]
            state[g] += dot(
                jnp.concatenate(left, axis=0), jnp.concatenate(right, axis=0), ((0,), (0,)))

    def row_of(j):
        return [(j, s) for s in range(1 if j == 0 else 0, n_inner)]

    def arrive_l(j):
        for s in others:

            @pl.when(z >= j)
            def _():
                l_across(n_inner - s, j).wait_recv()

    def arrive(j):
        for s in others:
            @pl.when((x + s >= n_inner) if j == 0 else (z >= j))
            def _():
                piece_across(n_inner - s, j).wait_recv()


    def visibility():
        list_copy.wait()
        lane = iota((1, keys_all), 1)
        key_block = (
            ((z - lane // tokens) * n_inner + x) * per_piece + lax.rem(lane, tokens) // BLK
        )
        listed = list_ref[...]
        for b in range(per_piece):
            member = key_block == listed[b:b + 1, 0:1]
            for i in range(1, listed.shape[1]):
                member = jnp.logical_or(member, key_block == listed[b:b + 1, i:i + 1])
            vis[b:b + 1, :] = jnp.where(member, 0.0, NEVER)

    def take_queries():
        q_copy.wait()
        qf = qbuf[...].astype(F32)
        for g in range(kv):
            qs[g] = qf[:, g * rep:(g + 1) * rep, :].reshape(rows, width).astype(BF16)

    half = BLK * rep
    scale = width ** (-0.5) * LOG2E

    def shown(s, j):
        cut = slice(j * tokens, (j + 1) * tokens)
        return jnp.concatenate(
            [s[b * half:(b + 1) * half] * scale + vis[b:b + 1, cut] for b in range(per_piece)],
            axis=0)

    def own_piece(g):
        plain = dot(qs[g], seg[0, 0, g], ((1,), (1,)))
        past = iota((rows, tokens), 0) // rep >= iota((rows, tokens), 1)
        score[g, :, 0:tokens] = jnp.where(past, shown(plain, 0), NEVER)
        hi, lo = halves(plain * spread_rows(wmat[g]))
        v_g = seg[0, 1, g]
        lin[g] = dot(
            jnp.concatenate([hi, lo], axis=1), jnp.concatenate([v_g, v_g], axis=0))

    def score_piece(j):
        for g in range(kv):
            s = dot(qs[g], seg[j, 0, g], ((1,), (1,)))
            score[g, :, j * tokens:(j + 1) * tokens] = shown(s, j)

    def weigh(g, at):
        s = score[g, at, :]
        top = jnp.max(s, axis=1, keepdims=True)
        expo = jnp.exp2(s - top)
        denom = jnp.sum(expo, axis=1, keepdims=True)
        prob[g, at, :] = expo.astype(BF16)
        inv[g, at, :] = jnp.broadcast_to(1.0 / denom, (s.shape[0], width))

    def sparse(g):
        v_g = jnp.concatenate([seg[j, 1, g] for j in range(n_seq)], axis=0)
        sp[g] = dot(prob[g], v_g) * inv[g]

    decays()
    take_queries()
    visibility()
    for g in range(kv):
        own_piece(g)

    weighing = [
        functools.partial(weigh, g, slice(b * half, (b + 1) * half))
        for g in range(kv) for b in range(per_piece)
    ]
    for j in range(1, n_seq):
        relay_l(j)
        for c in range(cuts[0]):
            relay_part(j, 0, c)
        arrive_l(j - 1)
        score_piece(j)
        weigh_pieces(row_of(j - 1))
        for c in range(cuts[1]):
            relay_part(j, 1, c)
            if j == last and weighing:
                weighing.pop(0)()
        if j > 1:
            arrive(j - 2)
            absorb(row_of(j - 2))
    for item in weighing:
        item()
    for g in range(kv):
        sparse(g)
    if n_seq > 1:
        arrive(last - 1)
        absorb(row_of(last - 1))
    g_copy.wait()
    gains = gain_ref[...] * width ** 0.5

    for j in range(last):

        @pl.when((z >= j) & has_next)
        def _():
            piece_hop(j).wait_send()
            l_hop(j).wait_send()

    for o in others:
        for j in range(last):

            @pl.when(z >= j)
            def _():
                l_across(o, j).wait_send()

            @pl.when((x + o < n_inner) if j == 0 else (z >= j))
            def _():
                piece_across(o, j).wait_send()

    arrive_l(last)
    weigh_pieces(row_of(last))
    arrive(last)
    absorb(row_of(last))

    done = []
    for g in range(kv):
        hi, lo = halves(state[g])
        q_g = qs[g]
        inter = dot(
            jnp.concatenate([q_g, q_g], axis=1), jnp.concatenate([hi, lo], axis=0))
        linear = lin[g] + inter * emat[g]
        norm = lax.rsqrt(jnp.sum(linear * linear, axis=1, keepdims=True) + width * 1e-6)
        scaled = (linear * norm).reshape(tokens, rep, width) * gains[g * rep:(g + 1) * rep, :][None]
        done.append(scaled + sp[g].reshape(tokens, rep, width))
    out_ref[...] = jnp.concatenate(done, axis=1).astype(out_ref.dtype)

    for o in others:

        @pl.when(z >= last)
        def _():
            l_across(o, last).wait_send()
            piece_across(o, last).wait_send()


def shards(n_seq, n_inner, queries, keys, values, log_decay, gain, block_list):
    tokens, heads, width = queries.shape
    kv = keys.shape[1]
    rows = tokens * (heads // kv)
    pairs = tokens * kv
    keys_all = n_seq * tokens
    cuts = (kv, 2 * kv) if n_seq * n_inner <= 16 else (1, 1)
    side = max(n_inner - 1, 1)
    anywhere = pl.BlockSpec(memory_space=pl.ANY)
    dma = pltpu.SemaphoreType.DMA
    return pl.pallas_call(
        functools.partial(kernel, n_seq, n_inner, kv, cuts),
        out_shape=pltpu.VMEM(queries.shape, queries.dtype),
        in_specs=[anywhere] * 6,
        out_specs=pl.BlockSpec(memory_space=pltpu.VMEM),
        scratch_shapes=[
            pltpu.VMEM(gain.shape, F32),
            pltpu.VMEM(block_list.shape, jnp.int32),
            pltpu.VMEM(queries.shape, BF16),
            pltpu.VMEM((2, pairs, width), BF16),
            pltpu.VMEM((n_seq, 2, kv, tokens, width), BF16),
            pltpu.VMEM((side, n_seq, 2, kv, tokens, width), BF16),
            pltpu.VMEM((n_seq, n_inner, LD_ROWS, tokens), F32),
            pltpu.VMEM((kv, rows, width), BF16),
            pltpu.VMEM((block_list.shape[0], keys_all), F32),
            pltpu.VMEM((kv, tokens, tokens), F32),
            pltpu.VMEM((kv, rows, width), F32),
            pltpu.VMEM((3, n_inner, kv, tokens, width), F32),
            pltpu.VMEM((kv, rows, keys_all), F32),
            pltpu.VMEM((kv, rows, keys_all), BF16),
            pltpu.VMEM((kv, rows, width), F32),
            pltpu.VMEM((kv, rows, width), F32),
            pltpu.VMEM((kv, rows, width), F32),
            pltpu.VMEM((kv, width, width), F32),
            dma((6,)),
            dma((n_seq, cuts[0])), dma((n_seq, cuts[1])), dma((n_seq,)),
            dma((n_seq,)), dma((n_seq,)), dma((n_inner, n_seq)), dma((n_inner, n_seq)),
            dma((n_inner, n_seq)), dma((n_inner, n_seq)),
        ],
        compiler_params=pltpu.CompilerParams(collective_id=0, has_side_effects=True),
        name="prefill",
    )(
        queries, keys.reshape(pairs, width), values.reshape(pairs, width),
        log_decay.T, gain, block_list,
    )


def solution(mesh):
    return jax.shard_map(
        functools.partial(shards, mesh.shape["seq"], mesh.shape["inner"]),
        mesh=mesh,
        in_specs=(
            P(("groups", "seq", "inner"), "head", None),
            P(("groups", "seq", "inner"), "head", None),
            P(("groups", "seq", "inner"), "head", None),
            P(("groups", "seq", "inner"), "head"),
            P("head", None),
            P(("groups", "seq", "inner"), None),
        ),
        out_specs=P(("groups", "seq", "inner"), "head", None),
        check_vma=False,
    )
```

time: 18.9 us -> 17.3 us (0.915)
  Pallas kernels: 18 us -> 16.3 us
    pallas_call x1, Pallas kernels: 18 us -> 16.3 us  [shards(): pl.pallas_call(functools.partial(kernel, n_seq, n_inner, kv, cuts), out_s...]
where the time goes in v3:
time: 17.3 us; the launch traced here: 17.1 us
  Pallas kernels  16.3 us (94%)
  local copies, waits for them, and re-layouts  0.8 us (5%)
    pallas_call x1, Pallas kernels, shards(): pl.pallas_call(functools.partial(kernel, n_seq, n_inner, kv, cuts), out_s...  16.3 us
    unnamed x1, local copies, waits for them, and re-layouts  0.8 us

profile of v3, /device:TPU:24, one launch (start us, length us, event | category | flops | bytes accessed | tf_op | source)
XLA Modules:
  0.0 17.1 jit_solution(13905947431613830353)
XLA Ops:
  0.0 16.3 %prefill.1 = bf16[128,16,128]{2,1,0:T(8,128)(2,1)S(1)} custom-call(bf16[128,16,128]{2,1,0:T(8,128)(2,1)} %q_hbm.1, bf16[256,128]{1,0:T(8,128)(2,1)} %bitcast.3, bf16[256,128]{1,0:T(8,128)(2,1)} %bitcast.4, f32[2,128]{1,0:T(2,128)} %bitcast.5, f32[16,128]{1,0:T(8,128)} %gain_hbm.1, s32[2,16]{1,0:T(2,128)} %list_hbm.1), custom_call_target="tpu_custom_call" | custom-call | tf_op jit(solution)/shard_map/prefill/pallas_call | solution.py:421
  16.3 0.8 %copy.8 = bf16[128,16,128]{2,1,0:T(8,128)(2,1)} copy(bf16[128,16,128]{2,1,0:T(8,128)(2,1)S(1)} %prefill.1) | data formatting | bytes 1048576

commit v4 on v3

--- a/solution.py
+++ b/solution.py
@@ -114,29 +114,29 @@
     def part_hop(j, i, c):
         return hop(
             part(seg.at[j], i, c), part(seg.at[j + 1], i, c), h_send.at[j],
-            (k_recv, v_recv)[i].at[j + 1, c])
+            (k_recv, v_recv)[i].at[j, c])
 
     def piece_hop(j):
-        return hop(seg.at[j], seg.at[j + 1], h_send.at[j], k_recv.at[j + 1, 0])
+        return hop(seg.at[j], seg.at[j + 1], h_send.at[j], k_recv.at[j, 0])
 
     def l_hop(j):
         return hop(
-            ldbuf.at[j, 0, 0:kv], ldbuf.at[j + 1, 0, 0:kv], l_send.at[j], l_recv.at[j + 1])
+            ldbuf.at[j, 0, 0:kv], ldbuf.at[j + 1, 0, 0:kv], l_send.at[j], l_recv.at[j])
 
     def part_across(o, j, i, c):
         s = n_inner - o
         return across(
-            o, part(seg.at[j], i, c), part(cross.at[s - 1, j], i, c), c_send.at[o, j],
-            c_recv.at[s, j])
+            o, part(seg.at[j], i, c), part(cross.at[s - 1, j], i, c), c_send.at[o - 1, j],
+            c_recv.at[s - 1, j])
 
     def piece_across(o, j):
         s = n_inner - o
-        return across(o, seg.at[j], cross.at[s - 1, j], c_send.at[o, j], c_recv.at[s, j])
+        return across(o, seg.at[j], cross.at[s - 1, j], c_send.at[o - 1, j], c_recv.at[s - 1, j])
 
     def l_across(o, j):
         s = n_inner - o
         return across(
-            o, ldbuf.at[j, 0, 0:kv], ldbuf.at[j, s, 0:kv], x_send.at[o, j], x_recv.at[s, j])
+            o, ldbuf.at[j, 0, 0:kv], ldbuf.at[j, s, 0:kv], x_send.at[o - 1, j], x_recv.at[s - 1, j])
 
     def relay_part(j, i, c):
         @pl.when(z >= j)
@@ -350,18 +350,22 @@
         weigh_pieces(row_of(j - 1))
         for c in range(cuts[1]):
             relay_part(j, 1, c)
-            if j == last and weighing:
-                weighing.pop(0)()
+        if j == last:
+            for item in weighing:
+                item()
         if j > 1:
             arrive(j - 2)
             absorb(row_of(j - 2))
-    for item in weighing:
-        item()
+    if n_seq == 1:
+        for item in weighing:
+            item()
     for g in range(kv):
         sparse(g)
+    arrive_l(last)
+    weigh_pieces(row_of(last))
     if n_seq > 1:
         arrive(last - 1)
-        absorb(row_of(last - 1))
+        absorb(row_of(last - 1) + [(last, 0)])
     g_copy.wait()
     gains = gain_ref[...] * width ** 0.5
 
@@ -383,10 +387,8 @@
             def _():
                 piece_across(o, j).wait_send()
 
-    arrive_l(last)
-    weigh_pieces(row_of(last))
     arrive(last)
-    absorb(row_of(last))
+    absorb([(last, s) for s in others])
 
     done = []
     for g in range(kv):
@@ -415,7 +417,7 @@
     pairs = tokens * kv
     keys_all = n_seq * tokens
     cuts = (kv, 2 * kv) if n_seq * n_inner <= 16 else (1, 1)
-    side = max(n_inner - 1, 1)
+    side, hops = max(n_inner - 1, 1), max(n_seq - 1, 1)
     anywhere = pl.BlockSpec(memory_space=pl.ANY)
     dma = pltpu.SemaphoreType.DMA
     return pl.pallas_call(
@@ -443,9 +445,9 @@
             pltpu.VMEM((kv, rows, width), F32),
             pltpu.VMEM((kv, width, width), F32),
             dma((6,)),
-            dma((n_seq, cuts[0])), dma((n_seq, cuts[1])), dma((n_seq,)),
-            dma((n_seq,)), dma((n_seq,)), dma((n_inner, n_seq)), dma((n_inner, n_seq)),
-            dma((n_inner, n_seq)), dma((n_inner, n_seq)),
+            dma((hops, cuts[0])), dma((hops, cuts[1])), dma((hops,)),
+            dma((hops,)), dma((hops,)), dma((side, n_seq)), dma((side, n_seq)),
+            dma((side, n_seq)), dma((side, n_seq)),
         ],
         compiler_params=pltpu.CompilerParams(collective_id=0, has_side_effects=True),
         name="prefill",

time: 17.3 us -> 16.6 us (0.960)
  Pallas kernels: 16.3 us -> 15.6 us
    pallas_call x1, Pallas kernels: 16.3 us -> 15.6 us  [shards(): pl.pallas_call(functools.partial(kernel, n_seq, n_inner, kv, cuts), out_s...]
where the time goes in v4:
time: 16.6 us; the launch traced here: 16.5 us
  Pallas kernels  15.6 us (94%)
  local copies, waits for them, and re-layouts  0.8 us (5%)
    pallas_call x1, Pallas kernels, shards(): pl.pallas_call(functools.partial(kernel, n_seq, n_inner, kv, cuts), out_s...  15.6 us
    unnamed x1, local copies, waits for them, and re-layouts  0.8 us

profile of v4, /device:TPU:24, one launch (start us, length us, event | category | flops | bytes accessed | tf_op | source)
XLA Modules:
  0.0 16.5 jit_solution(11635849023395117746)
XLA Ops:
  0.0 15.6 %prefill.1 = bf16[128,16,128]{2,1,0:T(8,128)(2,1)S(1)} custom-call(bf16[128,16,128]{2,1,0:T(8,128)(2,1)} %q_hbm.1, bf16[256,128]{1,0:T(8,128)(2,1)} %bitcast.3, bf16[256,128]{1,0:T(8,128)(2,1)} %bitcast.4, f32[2,128]{1,0:T(2,128)} %bitcast.5, f32[16,128]{1,0:T(8,128)} %gain_hbm.1, s32[2,16]{1,0:T(2,128)} %list_hbm.1), custom_call_target="tpu_custom_call" | custom-call | tf_op jit(solution)/shard_map/prefill/pallas_call | solution.py:423
  15.7 0.8 %copy.8 = bf16[128,16,128]{2,1,0:T(8,128)(2,1)} copy(bf16[128,16,128]{2,1,0:T(8,128)(2,1)S(1)} %prefill.1) | data formatting | bytes 1048576

commit v5 on v4

--- a/solution.py
+++ b/solution.py
@@ -46,6 +46,7 @@
     gain_ref, list_ref, qbuf, raw, seg, cross, ldbuf, qs, vis, wmat, emat, cols,
     score, prob, inv, lin, sp, state,
     local_sem, k_recv, v_recv, h_send, l_send, l_recv, x_send, x_recv, c_send, c_recv,
+    a_send, a_recv,
 ):
     z = lax.axis_index("seq")
     x = lax.axis_index("inner")
@@ -58,6 +59,8 @@
     has_next, has_last = z < n_seq - 1, z > 0
     others = range(1, n_inner)
     last = n_seq - 1
+    around = last > 1
+    first = lax.axis_index("head") == 0
 
     barrier = pltpu.get_barrier_semaphore()
 
@@ -125,9 +128,31 @@
 
     def part_across(o, j, i, c):
         s = n_inner - o
+        recv = c_recv.at[s - 1, j]
+        if around and j == last - 1 and i == 0:
+            recv = a_recv.at[s - 1]
         return across(
-            o, part(seg.at[j], i, c), part(cross.at[s - 1, j], i, c), c_send.at[o - 1, j],
-            c_recv.at[s - 1, j])
+            o, part(seg.at[j], i, c), part(cross.at[s - 1, j], i, c), c_send.at[o - 1, j], recv)
+
+    def half_across(o, j, i, recv):
+        s = n_inner - o
+        return across(o, seg.at[j, i], cross.at[s - 1, j, i], c_send.at[o - 1, j], recv)
+
+    def keys_around(s):
+        return hop(
+            cross.at[s - 1, last - 1, 0], cross.at[s - 1, last, 0], a_send.at[s - 1],
+            c_recv.at[s - 1, last])
+
+    def send_around():
+        for s in others:
+
+            @pl.when(z == last - 1)
+            def _():
+                half_across(n_inner - s, last - 1, 0, a_recv.at[s - 1]).wait_recv()
+
+            @pl.when((z == last - 1) & first)
+            def _():
+                keys_around(s).start()
 
     def piece_across(o, j):
         s = n_inner - o
@@ -148,8 +173,10 @@
                 def _():
                     part_hop(j, i, c).start()
 
-            for o in others:
-                part_across(o, j, i, c).start()
+            @pl.when(jnp.logical_not(first) if around and j == last and i == 0 else z >= j)
+            def _():
+                for o in others:
+                    part_across(o, j, i, c).start()
 
     def relay_l(j):
         @pl.when(z >= j)
@@ -274,7 +301,15 @@
         for s in others:
             @pl.when((x + s >= n_inner) if j == 0 else (z >= j))
             def _():
-                piece_across(n_inner - s, j).wait_recv()
+                if around and j == last - 1:
+                    half_across(n_inner - s, j, 1, c_recv.at[s - 1, j]).wait_recv()
+
+                    @pl.when(z == last)
+                    def _():
+                        half_across(n_inner - s, j, 0, a_recv.at[s - 1]).wait_recv()
+
+                else:
+                    piece_across(n_inner - s, j).wait_recv()
 
 
     def visibility():
@@ -314,8 +349,8 @@
         lin[g] = dot(
             jnp.concatenate([hi, lo], axis=1), jnp.concatenate([v_g, v_g], axis=0))
 
-    def score_piece(j):
-        for g in range(kv):
+    def score_piece(j, those):
+        for g in those:
             s = dot(qs[g], seg[j, 0, g], ((1,), (1,)))
             score[g, :, j * tokens:(j + 1) * tokens] = shown(s, j)
 
@@ -334,6 +369,7 @@
     decays()
     take_queries()
     visibility()
+
     for g in range(kv):
         own_piece(g)
 
@@ -342,30 +378,46 @@
         for g in range(kv) for b in range(per_piece)
     ]
     for j in range(1, n_seq):
-        relay_l(j)
+        if j == 1 or j < last:
+            relay_l(j)
+        early = 0
         for c in range(cuts[0]):
             relay_part(j, 0, c)
+            if j == last > 1 and cuts[0] == kv:
+                if c == kv - 1:
+                    early = 1
+                    relay_part(j, 1, 0)
+                score_piece(j, [c])
         arrive_l(j - 1)
-        score_piece(j)
-        weigh_pieces(row_of(j - 1))
+        if early == 0:
+            score_piece(j, range(kv))
+        if j < last:
+            weigh_pieces(row_of(j - 1))
         for c in range(cuts[1]):
-            relay_part(j, 1, c)
+            if c >= early:
+                relay_part(j, 1, c)
+        if j == last - 1:
+            relay_l(last)
         if j == last:
+            if around:
+                send_around()
+            weigh_pieces(row_of(j - 1))
             for item in weighing:
                 item()
-        if j > 1:
+        if 1 < j < last:
             arrive(j - 2)
             absorb(row_of(j - 2))
     if n_seq == 1:
         for item in weighing:
             item()
+    if last > 1:
+        arrive(last - 2)
     for g in range(kv):
         sparse(g)
+    if last > 1:
+        absorb(row_of(last - 2) + [(last - 1, 0)])
     arrive_l(last)
     weigh_pieces(row_of(last))
-    if n_seq > 1:
-        arrive(last - 1)
-        absorb(row_of(last - 1) + [(last, 0)])
     g_copy.wait()
     gains = gain_ref[...] * width ** 0.5
 
@@ -376,6 +428,13 @@
             piece_hop(j).wait_send()
             l_hop(j).wait_send()
 
+    if around:
+
+        @pl.when((z == last - 1) & first)
+        def _():
+            for s in others:
+                keys_around(s).wait_send()
+
     for o in others:
         for j in range(last):
 
@@ -387,9 +446,12 @@
             def _():
                 piece_across(o, j).wait_send()
 
+    if last > 0:
+        arrive(last - 1)
+        absorb([(last - 1, s) for s in others if last > 0] + [(last, 0)])
+
     arrive(last)
     absorb([(last, s) for s in others])
-
     done = []
     for g in range(kv):
         hi, lo = halves(state[g])
@@ -407,7 +469,18 @@
         @pl.when(z >= last)
         def _():
             l_across(o, last).wait_send()
-            piece_across(o, last).wait_send()
+            if around:
+
+                @pl.when(first)
+                def _():
+                    half_across(o, last, 1, c_recv.at[n_inner - o - 1, last]).wait_send()
+
+                @pl.when(jnp.logical_not(first))
+                def _():
+                    piece_across(o, last).wait_send()
+
+            else:
+                piece_across(o, last).wait_send()
 
 
 def shards(n_seq, n_inner, queries, keys, values, log_decay, gain, block_list):
@@ -447,7 +520,7 @@
             dma((6,)),
             dma((hops, cuts[0])), dma((hops, cuts[1])), dma((hops,)),
             dma((hops,)), dma((hops,)), dma((side, n_seq)), dma((side, n_seq)),
-            dma((side, n_seq)), dma((side, n_seq)),
+            dma((side, n_seq)), dma((side, n_seq)), dma((side,)), dma((side,)),
         ],
         compiler_params=pltpu.CompilerParams(collective_id=0, has_side_effects=True),
         name="prefill",

time: 16.6 us -> 16.4 us (0.988)
  Pallas kernels: 15.6 us -> 15.4 us
    pallas_call x1, Pallas kernels: 15.6 us -> 15.4 us  [shards(): pl.pallas_call(functools.partial(kernel, n_seq, n_inner, kv, cuts), out_s...]
where the time goes in v5:
time: 16.4 us; the launch traced here: 16.2 us
  Pallas kernels  15.4 us (94%)
  local copies, waits for them, and re-layouts  0.8 us (5%)
    pallas_call x1, Pallas kernels, shards(): pl.pallas_call(functools.partial(kernel, n_seq, n_inner, kv, cuts), out_s...  15.4 us
    unnamed x1, local copies, waits for them, and re-layouts  0.8 us

profile of v5, /device:TPU:24, one launch (start us, length us, event | category | flops | bytes accessed | tf_op | source)
XLA Modules:
  0.0 16.2 jit_solution(7027577042873030714)
XLA Ops:
  0.0 15.4 %prefill.1 = bf16[128,16,128]{2,1,0:T(8,128)(2,1)S(1)} custom-call(bf16[128,16,128]{2,1,0:T(8,128)(2,1)} %q_hbm.1, bf16[256,128]{1,0:T(8,128)(2,1)} %bitcast.3, bf16[256,128]{1,0:T(8,128)(2,1)} %bitcast.4, f32[2,128]{1,0:T(2,128)} %bitcast.5, f32[16,128]{1,0:T(8,128)} %gain_hbm.1, s32[2,16]{1,0:T(2,128)} %list_hbm.1), custom_call_target="tpu_custom_call" | custom-call | tf_op jit(solution)/shard_map/prefill/pallas_call | solution.py:496
  15.4 0.8 %copy.8 = bf16[128,16,128]{2,1,0:T(8,128)(2,1)} copy(bf16[128,16,128]{2,1,0:T(8,128)(2,1)S(1)} %prefill.1) | data formatting | bytes 1048576

commit v6 on v4

--- a/solution.py
+++ b/solution.py
@@ -45,7 +45,7 @@
     out_ref,
     gain_ref, list_ref, qbuf, raw, seg, cross, ldbuf, qs, vis, wmat, emat, cols,
     score, prob, inv, lin, sp, state,
-    local_sem, k_recv, v_recv, h_send, l_send, l_recv, x_send, x_recv, c_send, c_recv,
+    local_sem, k_recv, v_recv, h_send, l_send, l_recv, x_send, x_recv, c_send, c_recv, a_send,
 ):
     z = lax.axis_index("seq")
     x = lax.axis_index("inner")
@@ -58,6 +58,10 @@
     has_next, has_last = z < n_seq - 1, z > 0
     others = range(1, n_inner)
     last = n_seq - 1
+    around = last > 2
+    first = lax.axis_index("head") == 0
+    turns = (z == last - 1) & first if around else z < 0
+    skips = (z == last) & first if around else z < 0
 
     barrier = pltpu.get_barrier_semaphore()
 
@@ -148,8 +152,13 @@
                 def _():
                     part_hop(j, i, c).start()
 
-            for o in others:
-                part_across(o, j, i, c).start()
+            @pl.when(jnp.logical_not(skips) if j == 1 else z >= j)
+            def _():
+                for o in others:
+                    part_across(o, j, i, c).start()
+
+    def piece_around(s):
+        return hop(cross.at[s - 1, 0], cross.at[s - 1, 1], a_send.at[s - 1], c_recv.at[s - 1, 1])
 
     def relay_l(j):
         @pl.when(z >= j)
@@ -174,13 +183,13 @@
     for o in others:
         l_across(o, 0).start()
 
-        @pl.when(x + o < n_inner)
+        @pl.when((x + o < n_inner) | turns)
         def _():
             piece_across(o, 0).start()
 
     for s in others:
 
-        @pl.when(x + s < n_inner)
+        @pl.when((x + s < n_inner) & jnp.logical_not(turns))
         def _():
             cross[s - 1, 0] = jnp.zeros_like(cross[s - 1, 0])
 
@@ -272,7 +281,7 @@
 
     def arrive(j):
         for s in others:
-            @pl.when((x + s >= n_inner) if j == 0 else (z >= j))
+            @pl.when((x + s >= n_inner) | turns if j == 0 else z >= j)
             def _():
                 piece_across(n_inner - s, j).wait_recv()
 
@@ -314,8 +323,8 @@
         lin[g] = dot(
             jnp.concatenate([hi, lo], axis=1), jnp.concatenate([v_g, v_g], axis=0))
 
-    def score_piece(j):
-        for g in range(kv):
+    def score_piece(j, those):
+        for g in those:
             s = dot(qs[g], seg[j, 0, g], ((1,), (1,)))
             score[g, :, j * tokens:(j + 1) * tokens] = shown(s, j)
 
@@ -334,6 +343,7 @@
     decays()
     take_queries()
     visibility()
+
     for g in range(kv):
         own_piece(g)
 
@@ -342,30 +352,49 @@
         for g in range(kv) for b in range(per_piece)
     ]
     for j in range(1, n_seq):
-        relay_l(j)
+        if j == 1 or j < last:
+            relay_l(j)
+        early = 0
         for c in range(cuts[0]):
             relay_part(j, 0, c)
+            if j == last > 1 and cuts[0] == kv:
+                if c == kv - 1:
+                    early = 1
+                    relay_part(j, 1, 0)
+                score_piece(j, [c])
         arrive_l(j - 1)
-        score_piece(j)
-        weigh_pieces(row_of(j - 1))
+        if early == 0:
+            score_piece(j, range(kv))
+        if j < last:
+            weigh_pieces(row_of(j - 1))
         for c in range(cuts[1]):
-            relay_part(j, 1, c)
+            if c >= early:
+                relay_part(j, 1, c)
+        if j == last - 1:
+            relay_l(last)
         if j == last:
+            weigh_pieces(row_of(j - 1))
             for item in weighing:
                 item()
-        if j > 1:
+        if 1 < j < last:
             arrive(j - 2)
+            if around and j == last - 1:
+
+                @pl.when(turns)
+                def _():
+                    for s in others:
+                        piece_around(s).start()
+
             absorb(row_of(j - 2))
     if n_seq == 1:
         for item in weighing:
             item()
     for g in range(kv):
         sparse(g)
+    if last > 1:
+        absorb([(j, 0) for j in range(max(last - 2, 1), last)])
     arrive_l(last)
     weigh_pieces(row_of(last))
-    if n_seq > 1:
-        arrive(last - 1)
-        absorb(row_of(last - 1) + [(last, 0)])
     g_copy.wait()
     gains = gain_ref[...] * width ** 0.5
 
@@ -375,6 +404,13 @@
         def _():
             piece_hop(j).wait_send()
             l_hop(j).wait_send()
+
+    if around:
+
+        @pl.when(turns)
+        def _():
+            for s in others:
+                piece_around(s).wait_send()
 
     for o in others:
         for j in range(last):
@@ -383,13 +419,20 @@
             def _():
                 l_across(o, j).wait_send()
 
-            @pl.when((x + o < n_inner) if j == 0 else (z >= j))
+            @pl.when(
+                (x + o < n_inner) | turns if j == 0
+                else (z >= j) & jnp.logical_not(skips) if j == 1 else z >= j)
             def _():
                 piece_across(o, j).wait_send()
 
+    if last > 0:
+        two = range(max(last - 2, 0), last)
+        for j in two:
+            arrive(j)
+        absorb([(j, s) for j in two for s in others] + [(last, 0)])
+
     arrive(last)
     absorb([(last, s) for s in others])
-
     done = []
     for g in range(kv):
         hi, lo = halves(state[g])
@@ -416,7 +459,7 @@
     rows = tokens * (heads // kv)
     pairs = tokens * kv
     keys_all = n_seq * tokens
-    cuts = (kv, 2 * kv) if n_seq * n_inner <= 16 else (1, 1)
+    cuts = (kv, kv) if n_seq * n_inner <= 16 else (1, 1)
     side, hops = max(n_inner - 1, 1), max(n_seq - 1, 1)
     anywhere = pl.BlockSpec(memory_space=pl.ANY)
     dma = pltpu.SemaphoreType.DMA
@@ -447,7 +490,7 @@
             dma((6,)),
             dma((hops, cuts[0])), dma((hops, cuts[1])), dma((hops,)),
             dma((hops,)), dma((hops,)), dma((side, n_seq)), dma((side, n_seq)),
-            dma((side, n_seq)), dma((side, n_seq)),
+            dma((side, n_seq)), dma((side, n_seq)), dma((side,)),
         ],
         compiler_params=pltpu.CompilerParams(collective_id=0, has_side_effects=True),
         name="prefill",

time: 16.6 us -> 16.5 us (level)
  no operation moved by 1% of the time
where the time goes in v6:
time: 16.5 us; the launch traced here: 16.3 us
  Pallas kernels  15.5 us (94%)
  local copies, waits for them, and re-layouts  0.8 us (5%)
    pallas_call x1, Pallas kernels, shards(): pl.pallas_call(functools.partial(kernel, n_seq, n_inner, kv, cuts), out_s...  15.5 us
    unnamed x1, local copies, waits for them, and re-layouts  0.8 us

profile of v6, /device:TPU:24, one launch (start us, length us, event | category | flops | bytes accessed | tf_op | source)
XLA Modules:
  0.0 16.3 jit_solution(3248884383997211085)
XLA Ops:
  0.0 15.5 %prefill.1 = bf16[128,16,128]{2,1,0:T(8,128)(2,1)S(1)} custom-call(bf16[128,16,128]{2,1,0:T(8,128)(2,1)} %q_hbm.1, bf16[256,128]{1,0:T(8,128)(2,1)} %bitcast.3, bf16[256,128]{1,0:T(8,128)(2,1)} %bitcast.4, f32[2,128]{1,0:T(2,128)} %bitcast.5, f32[16,128]{1,0:T(8,128)} %gain_hbm.1, s32[2,16]{1,0:T(2,128)} %list_hbm.1), custom_call_target="tpu_custom_call" | custom-call | tf_op jit(solution)/shard_map/prefill/pallas_call | solution.py:466
  15.5 0.8 %copy.8 = bf16[128,16,128]{2,1,0:T(8,128)(2,1)} copy(bf16[128,16,128]{2,1,0:T(8,128)(2,1)S(1)} %prefill.1) | data formatting | bytes 1048576
